TPU v7x, 32 devices: a whole 2x2x4 slice. The times are simulated.
32 devices in a mesh: layer: 4 (over y, x), row: 2 (over core), col: 4 (over z).
Axes of the slice: x: 2, y: 2, z: 4, core: 2. Of those that a mesh axis runs over, the one named last changes fastest.
Arguments:
- even_left: bfloat16 [2, 4, 32, 32, 256, 128], P(None, 'layer', 'row', 'col'), may hold values from -0.09375 to 0.09375
- even_right: bfloat16 [2, 4, 32, 32, 256, 128], P(None, 'layer', 'row', 'col'), may hold values from -0.25 to 0.25
- odd_left: bfloat16 [2, 4, 32, 32, 256, 128], P(None, 'layer', 'col', 'row'), may hold values from -0.09375 to 0.09375
- odd_right: bfloat16 [2, 4, 32, 32, 256, 128], P(None, 'layer', 'col', 'row'), may hold values from -0.25 to 0.25
- even_ranks: int32 [2, 4, 32, 32], P(None, 'layer', 'row', 'col'), may hold values from 16 to 64, as said below
- odd_ranks: int32 [2, 4, 32, 32], P(None, 'layer', 'col', 'row'), may hold values from 16 to 64, as said below
- even_sources: float32 [2, 4, 2, 8192, 128], P(None, 'layer', None, ('row', 'col')), may hold values from -6 to 6
- odd_sources: float32 [2, 4, 2, 8192, 128], P(None, 'layer', None, ('col', 'row')), may hold values from -6 to 6
Outputs:
- even_traces: float32 [4, 2, 8192, 128], P('layer', None, ('row', 'col'))
- odd_traces: float32 [4, 2, 8192, 128], P('layer', None, ('col', 'row'))
Inputs may be any that keep to these rules, and one draw needn't show every extreme that they name: `even_ranks`: every direction and pair has a tile of rank 64 and a tile of rank a quarter of 64. `odd_ranks`: every direction and pair has a tile of rank 64 and a tile of rank a quarter of 64.
All inputs are finite; a program needn't handle non-finite values.
Results may differ from a plain program's by a relative error of at most 0.008.
Values may be sent and summed in bfloat16 or wider, within the bound.
A program may use at most 256 MiB of HBM per device.

v0:
```python
import functools

import jax
import jax.numpy as jnp
from jax import lax
from jax.experimental import pallas as pl
from jax.experimental.pallas import tpu as pltpu
from jax.sharding import PartitionSpec as P

MESH = pl.DeviceIdType.MESH


def product_kernel(rows_per, flag_ref, rank_ref, x_ref, v_ref, u_ref, y_ref, xt_ref):
    step = pl.program_id(0)
    cols, tile, twice = v_ref.shape[3], v_ref.shape[4], v_ref.shape[5]
    width = x_ref.shape[1]
    half, batch = twice // 2, width // 2

    @pl.when(flag_ref[0] > 0)
    def _():
        @pl.when(step == 0)
        def _():
            for c in range(cols):
                block = x_ref[c * tile : (c + 1) * tile, :].astype(jnp.float32)
                xt_ref[c] = block.T.astype(jnp.bfloat16)

        lane = lax.broadcasted_iota(jnp.int32, (1, twice), 1)
        sign = jnp.where(lane < half, 1.0, -1.0).astype(jnp.float32)
        within = jnp.where(lane < half, lane, lane - half)
        group = 2 if cols % 2 == 0 else 1
        pair = 2 if rows_per % 2 == 0 else 1
        for a in range(0, rows_per, pair):
            totals = [jnp.zeros((width, tile), jnp.float32) for _ in range(pair)]
            for c in range(0, cols, group):
                stacked = [[None] * group for _ in range(pair)]
                for g in range(group):
                    right = jnp.concatenate([v_ref[0, 0, a + j, c + g] for j in range(pair)], axis=1)
                    coeff = jnp.dot(xt_ref[c + g], right, preferred_element_type=jnp.float32)
                    for j in range(pair):
                        rank = rank_ref[(step * rows_per + a + j) * cols + c + g]
                        mask = (within < rank).astype(jnp.float32)
                        part = coeff[:, j * twice : (j + 1) * twice]
                        top = (part[:batch] * sign - pltpu.roll(part[batch:], half, 1)) * mask
                        low = pltpu.roll(top, half, 1) * (-sign)
                        stacked[j][g] = jnp.concatenate([top, low], axis=0).astype(jnp.bfloat16)
                for j in range(pair):
                    left = jnp.concatenate([u_ref[0, 0, a + j, c + g] for g in range(group)], axis=1)
                    totals[j] += lax.dot_general(
                        jnp.concatenate(stacked[j], axis=1),
                        left,
                        (((1,), (1,)), ((), ())),
                        preferred_element_type=jnp.float32,
                    )
            for j in range(pair):
                y_ref[(a + j) * tile : (a + j + 1) * tile, :] = totals[j].T.astype(y_ref.dtype)


def product(flag, ranks, x, right, left, direction):
    _, _, rows, cols, tile, twice = right.shape
    width = x.shape[1]
    rows_per = 2 if rows % 2 == 0 else 1

    def factor_map(i, flag_ref, rank_ref):
        return (direction, 0, jnp.where(flag_ref[0] > 0, i, 0), 0, 0, 0)

    factor = pl.BlockSpec((1, 1, rows_per, cols, tile, twice), factor_map)
    return pl.pallas_call(
        functools.partial(product_kernel, rows_per),
        out_shape=jax.ShapeDtypeStruct((rows * tile, width), jnp.bfloat16),
        grid_spec=pltpu.PrefetchScalarGridSpec(
            num_scalar_prefetch=2,
            grid=(rows // rows_per,),
            in_specs=[pl.BlockSpec(memory_space=pltpu.VMEM), factor, factor],
            out_specs=pl.BlockSpec((rows_per * tile, width), lambda i, f, r: (i, 0)),
            scratch_shapes=[pltpu.VMEM((cols, width, tile), jnp.bfloat16)],
        ),
        compiler_params=pltpu.CompilerParams(vmem_limit_bytes=50 * 1024 * 1024),
        cost_estimate=pl.CostEstimate(
            flops=4 * rows * cols * tile * twice * width,
            bytes_accessed=4 * rows * cols * tile * twice,
            transcendentals=0,
        ),
        name="tile_product",
    )(flag, ranks, x, right, left)


def peer(axis, offset):
    size = lax.axis_size(axis)
    return lax.rem(lax.axis_index(axis) + offset, size)


def exchange_kernel(spec, *refs):
    step, batches, segments, sides, use_y, edge, last = spec
    refs = list(refs)
    layer = lax.axis_index("layer")
    take = lambda count: [refs.pop(0) for _ in range(count)]
    y_refs = take(2) if use_y else [None, None]
    src_refs = take(2)
    total_outs = take(2)
    x_refs = [None, None] if last else take(2)
    src_bufs, landing, total_refs = take(2), take(2), take(2)
    out_sem = take(1)[0]
    hand = take(2) if edge and not last else [None, None]
    src_sem, rs_send, rs_recv = take(1)[0], take(2), take(2)
    ag_send, ag_recv = ([None, None], [None, None]) if last else (take(2), take(2))
    shift_send, shift_recv = take(2) if edge and not last else (None, None)

    plan = []
    for side in range(2):
        direction, rs_axis, ag_axis = sides[side]
        distance = layer if direction > 0 else segments - 1 - layer
        slot = step - distance
        active = (slot >= 0) & (slot < batches)
        have_y = active if edge else active & (distance > 0)
        sends = active & (distance < segments - 1)
        receives = (slot + 1 >= 0) & (slot + 1 < batches) & (distance > 0)
        plan.append((direction, rs_axis, ag_axis, slot, active, have_y, sends, receives))

    barrier = pltpu.get_barrier_semaphore()
    expect = 0
    for axis in ("row", "col"):
        for k in range(1, lax.axis_size(axis)):
            pl.semaphore_signal(
                barrier, inc=1, device_id={axis: peer(axis, k)}, device_id_type=MESH
            )
            expect += 1
    expect = jnp.int32(expect)
    if edge and not last:
        for direction, _, _, _, _, _, sends, receives in plan:

            @pl.when(receives)
            def _(direction=direction):
                pl.semaphore_signal(
                    barrier, inc=1, device_id={"layer": layer - direction}, device_id_type=MESH
                )

            expect = expect + jnp.where(sends, 1, 0)

    def total_copy(side):
        return pltpu.make_async_copy(total_refs[side], total_outs[side], out_sem.at[side])

    def source_copy(side):
        slot = plan[side][3]
        direction = 0 if plan[side][0] > 0 else 1
        return pltpu.make_async_copy(
            src_refs[side].at[direction, 0, slot], src_bufs[side], src_sem.at[side]
        )

    for side in range(2):

        @pl.when(plan[side][4])
        def _(side=side):
            source_copy(side).start()

    pl.semaphore_wait(barrier, expect)
    shard = src_bufs[0].shape[0]

    def rs_copy(side, k):
        target = peer(plan[side][1], k)
        return pltpu.make_async_remote_copy(
            src_ref=y_refs[side].at[pl.ds(pl.multiple_of(target * shard, shard), shard)],
            dst_ref=landing[side].at[k - 1],
            send_sem=rs_send[side].at[k - 1],
            recv_sem=rs_recv[side].at[k - 1],
            device_id={plan[side][1]: target},
            device_id_type=MESH,
        )

    def ag_own(side):
        own = lax.axis_index(plan[side][2])
        return x_refs[side].at[pl.ds(pl.multiple_of(own * shard, shard), shard)]

    def ag_copy(side, k):
        return pltpu.make_async_remote_copy(
            src_ref=ag_own(side),
            dst_ref=ag_own(side),
            send_sem=ag_send[side].at[k - 1],
            recv_sem=ag_recv[side].at[k - 1],
            device_id={plan[side][2]: peer(plan[side][2], k)},
            device_id_type=MESH,
        )

    def shift_copy(side):
        return pltpu.make_async_remote_copy(
            src_ref=hand[side],
            dst_ref=ag_own(side),
            send_sem=shift_send.at[side],
            recv_sem=shift_recv.at[side],
            device_id={"layer": layer + plan[side][0]},
            device_id_type=MESH,
        )

    def peers(axis):
        return range(1, lax.axis_size(axis))

    order = sorted(range(2), key=lambda side: 0 if sides[side][1] == "row" else 1)
    for side in order:
        if use_y:

            @pl.when(plan[side][5])
            def _(side=side):
                for k in peers(plan[side][1]):
                    rs_copy(side, k).start()

    for side in order:
        direction, rs_axis, ag_axis, slot, active, have_y, sends, receives = plan[side]

        @pl.when(active)
        def _(side=side):
            source_copy(side).wait()

        if use_y:

            @pl.when(have_y)
            def _(side=side, rs_axis=rs_axis):
                for k in peers(rs_axis):
                    rs_copy(side, k).wait_recv()
                own = pl.multiple_of(lax.axis_index(rs_axis) * shard, shard)
                value = src_bufs[side][...] + y_refs[side][pl.ds(own, shard), :].astype(jnp.float32)
                for k in peers(rs_axis):
                    value = value + landing[side][k - 1].astype(jnp.float32)
                total_refs[side][...] = value

            plain = active & jnp.logical_not(have_y)
        else:
            plain = active
        if edge:

            @pl.when(active)
            def _(side=side):
                total_copy(side).start()

        else:

            @pl.when(plain)
            def _(side=side):
                total_refs[side][...] = src_bufs[side][...]

            @pl.when(active)
            def _(side=side, ag_axis=ag_axis):
                total_copy(side).start()
                own = pl.multiple_of(lax.axis_index(ag_axis) * shard, shard)
                x_refs[side][pl.ds(own, shard), :] = total_refs[side][...].astype(jnp.bfloat16)
                for k in peers(ag_axis):
                    ag_copy(side, k).start()

        if edge and not last:

            @pl.when(sends)
            def _(side=side):
                hand[side][...] = total_refs[side][...].astype(jnp.bfloat16)
                shift_copy(side).start()

    if edge and not last:
        for side in order:

            @pl.when(plan[side][7])
            def _(side=side):
                shift_copy(side).wait_recv()
                for k in peers(plan[side][2]):
                    ag_copy(side, k).start()

    for side in order:

        @pl.when(plan[side][4])
        def _(side=side):
            total_copy(side).wait()

        if use_y:

            @pl.when(plan[side][5])
            def _(side=side):
                for k in peers(plan[side][1]):
                    rs_copy(side, k).wait_send()

        if last:
            continue
        if edge:

            @pl.when(plan[side][6])
            def _(side=side):
                shift_copy(side).wait_send()

        @pl.when(plan[side][7] if edge else plan[side][4])
        def _(side=side):
            for k in peers(plan[side][2]):
                ag_copy(side, k).wait()


def exchange(step, edge, last, y_pair, src_pair, collective_id):
    batches = src_pair[0].shape[2]
    shard, width = src_pair[0].shape[3:]
    segments = lax.axis_size("layer")
    if edge:
        sides = ((1, "row", "row"), (-1, "col", "col"))
    else:
        sides = ((1, "col", "col"), (-1, "row", "row"))
    use_y = y_pair is not None
    spec = (step, batches, segments, sides, use_y, edge, last)
    operands = (list(y_pair) if use_y else []) + list(src_pair)
    vmem = pl.BlockSpec(memory_space=pltpu.VMEM)
    anywhere = pl.BlockSpec(memory_space=pltpu.HBM)
    in_specs = ([vmem] * 2 if use_y else []) + [anywhere] * 2
    outs = [jax.ShapeDtypeStruct((shard, width), jnp.float32)] * 2
    if not last:
        outs += [
            jax.ShapeDtypeStruct((lax.axis_size(side[2]) * shard, width), jnp.bfloat16)
            for side in sides
        ]
    count = [max(lax.axis_size(side[1]) - 1, 1) for side in sides]
    scratch = [pltpu.VMEM((shard, width), jnp.float32)] * 2
    scratch += [pltpu.VMEM((n, shard, width), jnp.bfloat16) for n in count]
    scratch += [pltpu.VMEM((shard, width), jnp.float32)] * 2
    scratch += [pltpu.SemaphoreType.DMA((2,))]
    if edge and not last:
        scratch += [pltpu.VMEM((shard, width), jnp.bfloat16)] * 2
    scratch += [pltpu.SemaphoreType.DMA((2,))]
    scratch += [pltpu.SemaphoreType.DMA((n,)) for n in count] * 2
    if not last:
        scratch += [pltpu.SemaphoreType.DMA((n,)) for n in count] * 2
    if edge and not last:
        scratch += [pltpu.SemaphoreType.DMA((2,))] * 2
    return pl.pallas_call(
        functools.partial(exchange_kernel, spec),
        out_shape=outs,
        in_specs=in_specs,
        out_specs=[anywhere] * 2 + [vmem] * (len(outs) - 2),
        scratch_shapes=scratch,
        compiler_params=pltpu.CompilerParams(
            collective_id=collective_id,
            has_side_effects=True,
            vmem_limit_bytes=50 * 1024 * 1024,
        ),
        name="exchange_edge" if edge else "exchange_mid",
    )(*operands)


def on_device(
    even_left, even_right, odd_left, odd_right, even_ranks, odd_ranks, even_sources, odd_sources
):
    segments = lax.axis_size("layer")
    layer = lax.axis_index("layer")
    batches = even_sources.shape[2]
    even_flat = [even_ranks[e, 0].reshape(-1) for e in range(2)]
    odd_flat = [odd_ranks[e, 0].reshape(-1) for e in range(2)]

    def flag(slot, skip):
        active = (slot >= 0) & (slot < batches) & jnp.logical_not(skip)
        return active.astype(jnp.int32).reshape(1)

    never = jnp.bool_(False)
    history = []
    x_down = x_up = None
    total_steps = batches + segments - 1
    for step in range(total_steps):
        down_slot = step - layer
        up_slot = step - (segments - 1 - layer)
        last = step + 1 == total_steps
        if step == 0:
            y_pair = None
        else:
            y_pair = (
                product(
                    flag(down_slot, layer == 0), even_flat[0], x_down, even_right, even_left, 0
                ),
                product(
                    flag(up_slot, layer == segments - 1), odd_flat[1], x_up, odd_right, odd_left, 1
                ),
            )
        down_even, up_odd, x_down, x_up = exchange(
            step, False, False, y_pair, (even_sources, odd_sources), 2 * step
        )
        y_pair = (
            product(flag(down_slot, never), odd_flat[0], x_down, odd_right, odd_left, 0),
            product(flag(up_slot, never), even_flat[1], x_up, even_right, even_left, 1),
        )
        result = exchange(step, True, last, y_pair, (odd_sources, even_sources), 2 * step + 1)
        down_odd, up_even = result[:2]
        if not last:
            x_down, x_up = result[2:]
        history.append((down_even, down_odd, up_even, up_odd))

    def chosen(which, batch, distance):
        picked = history[batch][which]
        for away in range(1, segments):
            picked = jnp.where(distance == away, history[batch + away][which], picked)
        return picked

    up_distance = segments - 1 - layer
    even_traces = jnp.stack(
        [chosen(0, m, layer) + chosen(2, m, up_distance) for m in range(batches)]
    )[None]
    odd_traces = jnp.stack(
        [chosen(1, m, layer) + chosen(3, m, up_distance) for m in range(batches)]
    )[None]
    return (even_traces, odd_traces)


def solution(mesh):
    in_specs = (
        P(None, "layer", "row", "col", None, None),
        P(None, "layer", "row", "col", None, None),
        P(None, "layer", "col", "row", None, None),
        P(None, "layer", "col", "row", None, None),
        P(None, "layer", "row", "col"),
        P(None, "layer", "col", "row"),
        P(None, "layer", None, ("row", "col"), None),
        P(None, "layer", None, ("col", "row"), None),
    )
    out_specs = (P("layer", None, ("row", "col"), None), P("layer", None, ("col", "row"), None))
    return jax.shard_map(
        on_device, mesh=mesh, in_specs=in_specs, out_specs=out_specs, check_vma=False
    )
```

profile of v0, /device:TPU:7, one launch (start us, length us, event | category | flops | bytes accessed | tf_op | source)
XLA Modules:
  0.0 532.2 jit_solution(13233000599848849245)
XLA Ops:
  1.5 5.6 %exchange_mid.5 = (f32[1024,128]{1,0:T(8,128)S(1)}, f32[1024,128]{1,0:T(8,128)S(1)}, bf16[4096,128]{1,0:T(8,128)(2,1)S(1)}, bf16[2048,128]{1,0:T(8,128)(2,1)S(1)}) custom-call(f32[2,1,2,1024,128]{4,3,2,1,0:T(8,128)} %refs_3_.17, f32[2,1,2,1024,128]{4,3,2,1,0:T(8,128)} %refs_2_.17), custom_call_target="tpu_custom_call" | custom-call | tf_op jit(solution)/shard_map/exchange_mid/pallas_call | solution.py:323
  7.2 13.5 %tile_product.19.refs_1_ = bf16[4096,128]{1,0:T(8,128)(2,1)S(1)} custom-call(s32[1]{0:T(128)} %bitcast.6.flag_ref, s32[128]{0:T(128)S(1)} %reshape_squeeze.14.rank_ref, bf16[2048,128]{1,0:T(8,128)(2,1)S(1)} %get-tuple-element.41.x_ref, bf16[2,1,16,8,256,128]{5,4,3,2,1,0:T(8,128)(2,1)} %v_ref.35, bf16[2,1,16,8,256,128]{5,4,3,2,1,0:T(8,128)(2,1)} %u_ref.35), custom_call_target="tpu_custom_call" | custom-call | flops 2147483648 | bytes 16777216 | tf_op jit(solution)/shard_map/tile_product/pallas_call | solution.py:67
  21.7 2.8 tile_product.18.refs_0_
  24.5 25.9 %exchange_edge.5 = (f32[1024,128]{1,0:T(8,128)S(1)}, f32[1024,128]{1,0:T(8,128)S(1)}, bf16[2048,128]{1,0:T(8,128)(2,1)S(1)}, bf16[4096,128]{1,0:T(8,128)(2,1)S(1)}) custom-call(bf16[2048,128]{1,0:T(8,128)(2,1)S(1)} %tile_product.18.refs_0_, bf16[4096,128]{1,0:T(8,128)(2,1)} %copy-done.1, f32[2,1,2,1024,128]{4,3,2,1,0:T(8,128)} %refs_2_.17, ...), custom_call_target="tpu_custom_call" | custom-call | tf_op jit(solution)/shard_map/exchange_edge/pallas_call | solution.py:323
  52.1 2.8 tile_product.21.refs_1_
  55.0 2.1 tile_product.20.refs_0_
  57.1 1.0 copy-done.7
  58.1 11.7 %exchange_mid.6 = (f32[1024,128]{1,0:T(8,128)S(1)}, f32[1024,128]{1,0:T(8,128)S(1)}, bf16[4096,128]{1,0:T(8,128)(2,1)S(1)}, bf16[2048,128]{1,0:T(8,128)(2,1)S(1)}) custom-call(bf16[4096,128]{1,0:T(8,128)(2,1)} %copy-done.7, bf16[2048,128]{1,0:T(8,128)(2,1)S(1)} %tile_product.21.refs_1_, f32[2,1,2,1024,128]{4,3,2,1,0:T(8,128)} %refs_3_.17, ...), custom_call_target="tpu_custom_call" | custom-call | tf_op jit(solution)/shard_map/exchange_mid/pallas_call | solution.py:323
  71.5 13.5 %tile_product.23.refs_1_ = bf16[4096,128]{1,0:T(8,128)(2,1)S(1)} custom-call(s32[1]{0:T(128)} %bitcast.8.flag_ref, s32[128]{0:T(128)S(1)} %reshape_squeeze.14.rank_ref, bf16[2048,128]{1,0:T(8,128)(2,1)S(1)} %get-tuple-element.45.x_ref, bf16[2,1,16,8,256,128]{5,4,3,2,1,0:T(8,128)(2,1)} %v_ref.35, bf16[2,1,16,8,256,128]{5,4,3,2,1,0:T(8,128)(2,1)} %u_ref.35), custom_call_target="tpu_custom_call" | custom-call | flops 2147483648 | bytes 16777216 | tf_op jit(solution)/shard_map/tile_product/pallas_call | solution.py:67
  85.9 2.8 tile_product.22.refs_0_
  88.7 62.0 %exchange_edge.6 = (f32[1024,128]{1,0:T(8,128)S(1)}, f32[1024,128]{1,0:T(8,128)S(1)}, bf16[2048,128]{1,0:T(8,128)(2,1)S(1)}, bf16[4096,128]{1,0:T(8,128)(2,1)S(1)}) custom-call(bf16[2048,128]{1,0:T(8,128)(2,1)S(1)} %tile_product.22.refs_0_, bf16[4096,128]{1,0:T(8,128)(2,1)} %copy-done.4, f32[2,1,2,1024,128]{4,3,2,1,0:T(8,128)} %refs_2_.17, ...), custom_call_target="tpu_custom_call" | custom-call | tf_op jit(solution)/shard_map/exchange_edge/pallas_call | solution.py:323
  152.3 2.1 tile_product.24.refs_0_
  155.4 2.8 tile_product.25.refs_1_
  158.2 7.8 %exchange_mid.7 = (f32[1024,128]{1,0:T(8,128)S(1)}, f32[1024,128]{1,0:T(8,128)S(1)}, bf16[4096,128]{1,0:T(8,128)(2,1)S(1)}, bf16[2048,128]{1,0:T(8,128)(2,1)S(1)}) custom-call(bf16[4096,128]{1,0:T(8,128)(2,1)} %copy-done.2, bf16[2048,128]{1,0:T(8,128)(2,1)S(1)} %tile_product.25.refs_1_, f32[2,1,2,1024,128]{4,3,2,1,0:T(8,128)} %refs_3_.17, ...), custom_call_target="tpu_custom_call" | custom-call | tf_op jit(solution)/shard_map/exchange_mid/pallas_call | solution.py:323
  167.6 2.1 tile_product.27.refs_1_
  170.7 2.8 tile_product.26.refs_0_
  173.4 140.4 %exchange_edge.7 = (f32[1024,128]{1,0:T(8,128)S(1)}, f32[1024,128]{1,0:T(8,128)S(1)}, bf16[2048,128]{1,0:T(8,128)(2,1)S(1)}, bf16[4096,128]{1,0:T(8,128)(2,1)S(1)}) custom-call(bf16[2048,128]{1,0:T(8,128)(2,1)S(1)} %tile_product.26.refs_0_, bf16[4096,128]{1,0:T(8,128)(2,1)} %copy-done.5, f32[2,1,2,1024,128]{4,3,2,1,0:T(8,128)} %refs_2_.17, ...), custom_call_target="tpu_custom_call" | custom-call | tf_op jit(solution)/shard_map/exchange_edge/pallas_call | solution.py:323
  315.4 13.5 %tile_product.28.refs_0_ = bf16[4096,128]{1,0:T(8,128)(2,1)S(1)} custom-call(s32[1]{0:T(128)} %bitcast.flag_ref, s32[128]{0:T(128)S(1)} %reshape_squeeze.12.rank_ref, bf16[2048,128]{1,0:T(8,128)(2,1)S(1)} %get-tuple-element.50.x_ref, bf16[2,1,16,8,256,128]{5,4,3,2,1,0:T(8,128)(2,1)} %v_ref.35, bf16[2,1,16,8,256,128]{5,4,3,2,1,0:T(8,128)(2,1)} %u_ref.35), custom_call_target="tpu_custom_call" | custom-call | flops 2147483648 | bytes 16777216 | tf_op jit(solution)/shard_map/tile_product/pallas_call | solution.py:67
  329.9 2.8 tile_product.29.refs_1_
  332.7 49.6 %exchange_mid.8 = (f32[1024,128]{1,0:T(8,128)S(1)}, f32[1024,128]{1,0:T(8,128)S(1)}, bf16[4096,128]{1,0:T(8,128)(2,1)S(1)}, bf16[2048,128]{1,0:T(8,128)(2,1)S(1)}) custom-call(bf16[4096,128]{1,0:T(8,128)(2,1)} %copy-done.3, bf16[2048,128]{1,0:T(8,128)(2,1)S(1)} %tile_product.29.refs_1_, f32[2,1,2,1024,128]{4,3,2,1,0:T(8,128)} %refs_3_.17, ...), custom_call_target="tpu_custom_call" | custom-call | tf_op jit(solution)/shard_map/exchange_mid/pallas_call | solution.py:323
  383.9 2.1 tile_product.31.refs_1_
  386.9 13.4 %tile_product.30.refs_0_ = bf16[2048,128]{1,0:T(8,128)(2,1)S(1)} custom-call(s32[1]{0:T(128)} %bitcast.12.flag_ref, s32[128]{0:T(128)S(1)} %reshape_squeeze.13.rank_ref, bf16[4096,128]{1,0:T(8,128)(2,1)S(1)} %get-tuple-element.56.x_ref, bf16[2,1,8,16,256,128]{5,4,3,2,1,0:T(8,128)(2,1)} %v_ref.34, bf16[2,1,8,16,256,128]{5,4,3,2,1,0:T(8,128)(2,1)} %u_ref.34), custom_call_target="tpu_custom_call" | custom-call | flops 2147483648 | bytes 16777216 | tf_op jit(solution)/shard_map/tile_product/pallas_call | solution.py:67
  400.4 35.4 %exchange_edge.8 = (f32[1024,128]{1,0:T(8,128)S(1)}, f32[1024,128]{1,0:T(8,128)S(1)}, bf16[2048,128]{1,0:T(8,128)(2,1)S(1)}, bf16[4096,128]{1,0:T(8,128)(2,1)S(1)}) custom-call(bf16[2048,128]{1,0:T(8,128)(2,1)S(1)} %tile_product.30.refs_0_, bf16[4096,128]{1,0:T(8,128)(2,1)} %copy-done.6, f32[2,1,2,1024,128]{4,3,2,1,0:T(8,128)} %refs_2_.17, ...), custom_call_target="tpu_custom_call" | custom-call | tf_op jit(solution)/shard_map/exchange_edge/pallas_call | solution.py:323
  437.3 13.5 %tile_product.32.refs_0_ = bf16[4096,128]{1,0:T(8,128)(2,1)S(1)} custom-call(s32[1]{0:T(128)} %bitcast.15.flag_ref, s32[128]{0:T(128)S(1)} %reshape_squeeze.12.rank_ref, bf16[2048,128]{1,0:T(8,128)(2,1)S(1)} %get-tuple-element.62.x_ref, bf16[2,1,16,8,256,128]{5,4,3,2,1,0:T(8,128)(2,1)} %v_ref.35, bf16[2,1,16,8,256,128]{5,4,3,2,1,0:T(8,128)(2,1)} %u_ref.35), custom_call_target="tpu_custom_call" | custom-call | flops 2147483648 | bytes 16777216 | tf_op jit(solution)/shard_map/tile_product/pallas_call | solution.py:67
  451.8 2.8 tile_product.33.refs_1_
  454.5 43.6 %exchange_mid.9 = (f32[1024,128]{1,0:T(8,128)S(1)}, f32[1024,128]{1,0:T(8,128)S(1)}, bf16[4096,128]{1,0:T(8,128)(2,1)S(1)}, bf16[2048,128]{1,0:T(8,128)(2,1)S(1)}) custom-call(bf16[4096,128]{1,0:T(8,128)(2,1)} %copy-done, bf16[2048,128]{1,0:T(8,128)(2,1)S(1)} %tile_product.33.refs_1_, f32[2,1,2,1024,128]{4,3,2,1,0:T(8,128)} %refs_3_.17, ...), custom_call_target="tpu_custom_call" | custom-call | tf_op jit(solution)/shard_map/exchange_mid/pallas_call | solution.py:323
  499.8 2.1 tile_product.35.refs_1_
  501.9 13.4 %tile_product.34.refs_0_ = bf16[2048,128]{1,0:T(8,128)(2,1)S(1)} custom-call(s32[1]{0:T(128)} %bitcast.17.flag_ref, s32[128]{0:T(128)S(1)} %reshape_squeeze.13.rank_ref, bf16[4096,128]{1,0:T(8,128)(2,1)S(1)} %get-tuple-element.65.x_ref, bf16[2,1,8,16,256,128]{5,4,3,2,1,0:T(8,128)(2,1)} %v_ref.34, bf16[2,1,8,16,256,128]{5,4,3,2,1,0:T(8,128)(2,1)} %u_ref.34), custom_call_target="tpu_custom_call" | custom-call | flops 2147483648 | bytes 16777216 | tf_op jit(solution)/shard_map/tile_product/pallas_call | solution.py:67
  515.3 10.7 %exchange_edge.9 = (f32[1024,128]{1,0:T(8,128)S(1)}, f32[1024,128]{1,0:T(8,128)S(1)}) custom-call(bf16[2048,128]{1,0:T(8,128)(2,1)S(1)} %tile_product.34.refs_0_, bf16[4096,128]{1,0:T(8,128)(2,1)S(1)} %tile_product.35.refs_1_, f32[2,1,2,1024,128]{4,3,2,1,0:T(8,128)} %refs_2_.17, f32[2,1,2,1024,128]{4,3,2,1,0:T(8,128)} %refs_3_.17), custom_call_target="tpu_custom_call" | custom-call | tf_op jit(solution)/shard_map/exchange_edge/pallas_call | solution.py:323
  526.1 2.2 add_bitcast_fusion.1
  528.3 2.4 add_bitcast_fusion.3
  530.7 1.5 maximum_bitcast_fusion
  (61 shorter events, 20.8 us)
Async XLA Ops:
  7.1 13.5 %copy-start.8 = (f32[1024,128]{1,0:T(8,128)}, f32[1024,128]{1,0:T(8,128)S(1)}, u32[]{:S(2)}) copy-start(f32[1024,128]{1,0:T(8,128)S(1)} %get-tuple-element.75) | copy-start | bytes 1572868
  7.2 14.5 %copy-start.26 = (s32[2,1,8,16]{3,2,1,0:T(8,128)S(1)}, s32[2,1,8,16]{3,2,1,0:T(8,128)}, u32[]{:S(2)}) copy-start(s32[2,1,8,16]{3,2,1,0:T(8,128)} %param.13) | copy-start | bytes 3076
  20.7 1.0 copy-start.1
  50.4 0.8 copy-start.10
  51.2 0.8 copy-start.11
  57.1 1.0 copy-start.7
  69.9 0.8 copy-start.12
  70.7 0.8 copy-start.14
  84.9 1.0 copy-start.4
  150.7 0.8 copy-start.13
  151.5 0.8 copy-start.15
  154.4 1.0 copy-start.2
  166.0 0.8 copy-start.16
  166.8 0.8 copy-start.18
  169.7 1.0 copy-start.5
  313.8 0.8 copy-start.17
  314.6 0.8 copy-start.19
  328.9 1.0 copy-start.3
  382.3 0.8 copy-start.20
  383.1 0.8 copy-start.22
  385.9 1.0 copy-start.6
  435.7 0.8 copy-start.21
  436.5 0.8 copy-start.23
  450.8 1.0 copy-start
  498.1 0.8 copy-start.24
  498.9 0.9 copy-start.25
  501.9 24.2 %copy-start.9 = (f32[1024,128]{1,0:T(8,128)S(1)}, f32[1024,128]{1,0:T(8,128)}, u32[]{:S(2)}) copy-start(f32[1024,128]{1,0:T(8,128)} %copy-done.8) | copy-start | bytes 1572868
where the time goes:
time: 540 us; the launch traced here: 532 us
  Pallas kernels  503 us (93%)
  local copies, waits for them, and re-layouts  21.7 us (4%)
  other arithmetic  6.1 us (1%)
    pallas_call x10, Pallas kernels, exchange(): pl.pallas_call(functools.partial(exchange_kernel, spec), out_shape=outs,...  393 us
    pallas_call x18, Pallas kernels, product(): pl.pallas_call(functools.partial(product_kernel, rows_per), out_shape=jax...  111 us
    unnamed x54, local copies, waits for them, and re-layouts  20.6 us

commit v1 on v0

v1 whole, which is shorter than its diff:
```python
import functools

import jax
import jax.numpy as jnp
from jax import lax
from jax.experimental import pallas as pl
from jax.experimental.pallas import tpu as pltpu
from jax.sharding import PartitionSpec as P

MESH = pl.DeviceIdType.MESH
F32, BF16 = jnp.float32, jnp.bfloat16
SKEW = 2


def sizes(right, sources):
    _, _, rows, cols, tile, twice = right.shape
    batches, shard, width = sources.shape[2:]
    return rows, cols, tile, twice, batches, shard, width, min(tile, shard)


def step_of(count):
    return 2 if count % 2 == 0 else 1


def sweep_kernel(
    erank, orank, eleft, eright, oleft, oright, esrc, osrc, eout, oout,
    ev, eu, ov, ou, se, so, a_recv, b_recv, a_send, b_send, part, x_local, x_odd, x_hand, x_even,
    acc, rs_send, rs_recv, hand,
    le_sem, lo_sem, src_sem, as_sem, bs_sem, ar_sem, br_sem, us_sem, ur_sem, hs_sem, hr_sem,
    gs_sem, gr_sem, rss_sem, rsr_sem,
):
    rows_e, cols_e, tile, twice, batches, shard, width, chunk = sizes(eright, esrc)
    rows_o, cols_o = oright.shape[2:4]
    half, batch = twice // 2, width // 2
    q = tile // chunk
    own = shard // chunk
    je, jo = rows_e * q, rows_o * q
    pe, po = step_of(rows_e), step_of(cols_o)
    pr, gc = step_of(rows_o), step_of(cols_e)
    segments, peers, line = (lax.axis_size(axis) for axis in ("layer", "row", "col"))
    p, r, i = (lax.axis_index(axis) for axis in ("layer", "row", "col"))
    first = jnp.where(2 * p <= segments - 1, 0, 1)
    has_e = lambda way: jnp.logical_or(way == 1, p > 0)
    has_o = lambda way: jnp.logical_or(way == 0, p < segments - 1)

    barrier = pltpu.get_barrier_semaphore()
    expect = jnp.int32(peers - 1)
    for k in range(1, peers):
        pl.semaphore_signal(barrier, inc=1, device_id={"row": lax.rem(r + k, peers)}, device_id_type=MESH)
    for axis, at, size in (("col", i, line), ("layer", p, segments)):
        for ok, to in ((at > 0, at - 1), (at < size - 1, at + 1)):

            @pl.when(ok)
            def _(axis=axis, to=to):
                pl.semaphore_signal(barrier, inc=1, device_id={axis: to}, device_id_type=MESH)

            expect = expect + jnp.where(ok, 1, 0)

    def src_copy(parity, way, m):
        ref, buf = ((esrc, se), (osrc, so))[parity]
        return pltpu.make_async_copy(ref.at[way, 0, m], buf.at[way, m], src_sem.at[parity, way, m])

    def load_e(way, t):
        at = pl.ds(t * pe, pe)
        return [
            pltpu.make_async_copy(ref.at[way, 0, at], buf.at[at], le_sem.at[n, t])
            for n, (ref, buf) in enumerate(((eright, ev), (eleft, eu)))
        ]

    def load_o(way, t):
        at = pl.ds(t * po, po)
        return [
            pltpu.make_async_copy(ref.at[way, 0, :, at], buf.at[:, at], lo_sem.at[n, t])
            for n, (ref, buf) in enumerate(((oright, ov), (oleft, ou)))
        ]

    def load_all(which, way):
        load, count = ((load_e, rows_e // pe), (load_o, cols_o // po))[which]

        @pl.loop(0, count)
        def _(t):
            for copy in load(way, t):
                copy.start()

    for parity in range(2):
        for way in range(2):
            for m in range(batches):
                src_copy(parity, way, m).start()
    second = 1 - first
    for turn in range(2):
        for which, has in ((0, has_e), (1, has_o)):
            now = (first == which) if turn == 0 else (first != which)

            @pl.when(now & has(first))
            def _(which=which):
                load_all(which, first)

            @pl.when(now & jnp.logical_not(has(first)) & has(second))
            def _(which=which):
                load_all(which, second)

    pl.semaphore_wait(barrier, expect)

    lane = lax.broadcasted_iota(jnp.int32, (1, twice), 1)
    sign = jnp.where(lane < half, 1.0, -1.0).astype(F32)
    within = jnp.where(lane < half, lane, lane - half)

    def stacked_of(coeff, rank):
        mask = (within < rank).astype(F32)
        top = (coeff[:batch] * sign - pltpu.roll(coeff[batch:], half, 1)) * mask
        low = pltpu.roll(top, half, 1) * (-sign)
        return jnp.concatenate([top, low], axis=0).astype(BF16)

    def tile_of(load, t):
        pieces = [load(t * q + n) for n in range(q)]
        return pieces[0] if q == 1 else jnp.concatenate(pieces, axis=1)

    def source_t(buf, way, m, t):
        return buf[way, m, pl.ds(pl.multiple_of(t * chunk, chunk), chunk), :].T

    def keep(out, turn, m, t, value):
        at = pl.ds(pl.multiple_of(t * chunk, chunk), chunk)

        @pl.when(turn == 0)
        def _():
            out[0, m, at, :] = value.T

        @pl.when(turn != 0)
        def _():
            out[0, m, at, :] = out[0, m, at, :] + value.T

    def even_product(way, m, a):
        stacked = [[] for _ in range(pe)]
        for c in range(cols_e):
            right = jnp.concatenate([ev[a + j, c] for j in range(pe)], axis=1)
            x = tile_of(lambda n: x_even[way, m, n], c)
            coeff = jnp.dot(x, right, preferred_element_type=F32)
            for j in range(pe):
                rank = erank[(way * rows_e + a + j) * cols_e + c]
                stacked[j].append(stacked_of(coeff[:, j * twice : (j + 1) * twice], rank))
        for j in range(pe):
            total = lax.dot_general(
                jnp.concatenate(stacked[j], axis=1),
                jnp.concatenate([eu[a + j, c] for c in range(cols_e)], axis=1),
                (((1,), (1,)), ((), ())),
                preferred_element_type=F32,
            )
            for n in range(q):
                part[(a + j) * q + n] = total[:, n * chunk : (n + 1) * chunk]

    def odd_product(way, c, load):
        xs = [tile_of(load, c + g) for g in range(po)]
        for a in range(0, rows_o, pr):
            stacked = [[] for _ in range(pr)]
            for g in range(po):
                right = jnp.concatenate([ov[a + j, c + g] for j in range(pr)], axis=1)
                coeff = jnp.dot(xs[g], right, preferred_element_type=F32)
                for j in range(pr):
                    rank = orank[(way * rows_o + a + j) * cols_o + c + g]
                    stacked[j].append(stacked_of(coeff[:, j * twice : (j + 1) * twice], rank))
            for j in range(pr):
                total = lax.dot_general(
                    jnp.concatenate(stacked[j], axis=1),
                    jnp.concatenate([ou[a + j, c + g] for g in range(po)], axis=1),
                    (((1,), (1,)), ((), ())),
                    preferred_element_type=F32,
                )
                for n in range(q):
                    at = (a + j) * q + n
                    acc[at] = acc[at] + total[:, n * chunk : (n + 1) * chunk]

    def a_copy(k, j):
        return pltpu.make_async_remote_copy(
            src_ref=a_send.at[j], dst_ref=a_recv.at[k, j],
            send_sem=as_sem.at[j], recv_sem=ar_sem.at[k, j],
            device_id={"col": lax.rem(i + 1, line)}, device_id_type=MESH,
        )

    def b_copy(k, j):
        return pltpu.make_async_remote_copy(
            src_ref=b_send.at[j], dst_ref=b_recv.at[k, j],
            send_sem=bs_sem.at[j], recv_sem=br_sem.at[k, j],
            device_id={"col": lax.rem(i + line - 1, line)}, device_id_type=MESH,
        )

    def up_copy(m, j):
        return pltpu.make_async_remote_copy(
            src_ref=x_hand.at[j], dst_ref=x_odd.at[m, j],
            send_sem=us_sem.at[j], recv_sem=ur_sem.at[m, j],
            device_id={"layer": lax.rem(p + segments - 1, segments)}, device_id_type=MESH,
        )

    def down_copy(m, t):
        return pltpu.make_async_remote_copy(
            src_ref=hand.at[t], dst_ref=x_even.at[0, m, r * own + t],
            send_sem=hs_sem.at[t], recv_sem=hr_sem.at[m, t],
            device_id={"layer": lax.rem(p + 1, segments)}, device_id_type=MESH,
        )

    def gather_copy(k, way, m, t, d, source):
        slot = x_even.at[way, m, source * own + t]
        return pltpu.make_async_remote_copy(
            src_ref=slot, dst_ref=slot,
            send_sem=gs_sem.at[d - 1, t], recv_sem=gr_sem.at[k, d - 1, t],
            device_id={"row": lax.rem(r + d, peers)}, device_id_type=MESH,
        )

    def scatter_copy(k, d):
        return pltpu.make_async_remote_copy(
            src_ref=rs_send.at[d - 1], dst_ref=rs_recv.at[k, d - 1],
            send_sem=rss_sem.at[d - 1], recv_sem=rsr_sem.at[k, d - 1],
            device_id={"row": lax.rem(r + d, peers)}, device_id_type=MESH,
        )

    def even_part(way, k, turn, m):
        full = has_e(way)
        final = jnp.logical_and(way == 1, p == 0)

        def sends_a(at, o):
            need = jnp.logical_or(full, at >= o) & (jnp.logical_not(final) | (o > at))
            return need & (at >= 0) & (at < line - 1)

        def sends_b(at, o):
            need = jnp.logical_or(full, at <= o) & (jnp.logical_not(final) | (o < at))
            return need & (at > 0) & (at < line)

        src_copy(0, way, m).wait()

        @pl.when(full)
        def _():
            for t in range(own):
                if way == 0:
                    down_copy(m, t).wait_recv()
                for d in range(1, peers):
                    gather_copy(k, way, m, t, d, r).start()
            for t in range(own):
                for d in range(1, peers):
                    gather_copy(k, way, m, t, d, lax.rem(r + peers - d, peers)).wait_recv()

        @pl.when(jnp.logical_not(full))
        def _():
            @pl.loop(0, je)
            def _(j):
                part[j] = jnp.zeros((width, chunk), F32)

            for t in range(own):
                part[i * own + t] = source_t(se, way, m, t)

        behind = jnp.maximum(i, line - 1 - i)

        @pl.loop(0, je + SKEW * (line - 1))
        def _(s):
            @pl.when(full & (s < je) & (lax.rem(s, pe * q) == 0))
            def _():
                t = s // (pe * q)

                @pl.when(m == 0)
                def _():
                    for copy in load_e(way, t):
                        copy.wait()

                even_product(way, m, t * pe)

                @pl.when((k == batches - 1) & has_e(second))
                def _():
                    for copy in load_e(second, t):
                        copy.start()

                for n in range(pe * q):
                    mine = s + n - i * own

                    @pl.when((mine >= 0) & (mine < own))
                    def _(n=n, mine=mine):
                        part[s + n] = part[s + n] + source_t(se, way, m, mine)

            ja = s - SKEW * i

            @pl.when((ja >= 0) & (ja < je))
            def _():
                o = ja // own
                got, put = sends_a(i - 1, o), sends_a(i, o)

                @pl.when(got)
                def _():
                    a_copy(k, ja).wait_recv()

                @pl.when(put & got)
                def _():
                    a_send[ja] = (part[ja] + a_recv[k, ja].astype(F32)).astype(BF16)

                @pl.when(put & jnp.logical_not(got))
                def _():
                    a_send[ja] = part[ja].astype(BF16)

                @pl.when(put)
                def _():
                    a_copy(k, ja).start()

            jb = s - SKEW * (line - 1 - i)

            @pl.when((jb >= 0) & (jb < je))
            def _():
                o = jb // own
                got, put = sends_b(i + 1, o), sends_b(i, o)

                @pl.when(got)
                def _():
                    b_copy(k, jb).wait_recv()

                @pl.when(put & got)
                def _():
                    b_send[jb] = (part[jb] + b_recv[k, jb].astype(F32)).astype(BF16)

                @pl.when(put & jnp.logical_not(got))
                def _():
                    b_send[jb] = part[jb].astype(BF16)

                @pl.when(put)
                def _():
                    b_copy(k, jb).start()

            jt = s - SKEW * behind

            @pl.when((jt >= 0) & (jt < je))
            def _():
                o = jt // own
                mine = o == i

                @pl.when(jnp.logical_not(final) | mine)
                def _():
                    @pl.when(sends_a(i - 1, o))
                    def _():
                        part[jt] = part[jt] + a_recv[k, jt].astype(F32)

                    @pl.when(sends_b(i + 1, o))
                    def _():
                        part[jt] = part[jt] + b_recv[k, jt].astype(F32)

                @pl.when(mine)
                def _():
                    keep(eout, turn, m, jt - i * own, part[jt])

                if way == 0:
                    x_local[jt] = part[jt].astype(BF16)

                    @pl.when(lax.rem(jt, po * q) == po * q - 1)
                    def _():
                        odd_columns(way, k, m, jt // (po * q), lambda n: x_local[n])

                else:

                    @pl.when(jnp.logical_not(final))
                    def _():
                        x_hand[jt] = part[jt].astype(BF16)
                        up_copy(m, jt).start()

        @pl.when(full)
        def _():
            for t in range(own):
                for d in range(1, peers):
                    gather_copy(k, way, m, t, d, r).wait_send()

        @pl.loop(0, je)
        def _(j):
            o = j // own

            @pl.when(sends_a(i, o))
            def _():
                a_copy(k, j).wait_send()

            @pl.when(sends_b(i, o))
            def _():
                b_copy(k, j).wait_send()

            if way == 1:

                @pl.when(jnp.logical_not(final))
                def _():
                    up_copy(m, j).wait_send()

    def odd_columns(way, k, m, t, load):
        @pl.when(m == 0)
        def _():
            for copy in load_o(way, t):
                copy.wait()

        @pl.when(t == 0)
        def _():
            @pl.loop(0, jo)
            def _(j):
                acc[j] = jnp.zeros((width, chunk), F32)

        odd_product(way, t * po, load)

        @pl.when((k == batches - 1) & has_o(second))
        def _():
            for copy in load_o(second, t):
                copy.start()

    def odd_rest(way, k, turn, m):
        full = has_o(way)
        src_copy(1, way, m).wait()

        @pl.when(full)
        def _():
            for d in range(1, peers):
                target = lax.rem(r + d, peers)
                for t in range(own):
                    rs_send[d - 1, t] = acc[target * own + t].astype(BF16)
                scatter_copy(k, d).start()
            for d in range(1, peers):
                scatter_copy(k, d).wait_recv()
                for t in range(own):
                    at = r * own + t
                    acc[at] = acc[at] + rs_recv[k, d - 1, t].astype(F32)

        @pl.when(jnp.logical_not(full))
        def _():
            for t in range(own):
                acc[r * own + t] = jnp.zeros((width, chunk), F32)

        for t in range(own):
            at = r * own + t
            total = acc[at] + source_t(so, way, m, t)
            if way == 0:

                @pl.when(p < segments - 1)
                def _(t=t, total=total):
                    hand[t] = total.astype(BF16)
                    down_copy(m, t).start()

            else:
                x_even[way, m, at] = total.astype(BF16)
            keep(oout, turn, m, t, total)

        @pl.when(full)
        def _():
            for d in range(1, peers):
                scatter_copy(k, d).wait_send()

        if way == 0:

            @pl.when(p < segments - 1)
            def _():
                for t in range(own):
                    down_copy(m, t).wait_send()

    @pl.loop(0, 2 * batches)
    def _(k):
        turn, m = k // batches, lax.rem(k, batches)
        way = jnp.where(turn == 0, first, second)

        @pl.when(way == 0)
        def _():
            even_part(0, k, turn, m)
            odd_rest(0, k, turn, m)

        @pl.when(way == 1)
        def _():
            @pl.when(has_o(1))
            def _():
                @pl.loop(0, cols_o // po)
                def _(t):
                    for n in range(po * q):
                        up_copy(m, t * po * q + n).wait_recv()
                    odd_columns(1, k, m, t, lambda n: x_odd[m, n])

            odd_rest(1, k, turn, m)
            even_part(1, k, turn, m)


def on_device(even_left, even_right, odd_left, odd_right, even_ranks, odd_ranks, even_sources, odd_sources):
    rows_e, cols_e, tile, twice, batches, shard, width, chunk = sizes(even_right, even_sources)
    rows_o, cols_o = odd_right.shape[2:4]
    peers = lax.axis_size("row")
    q, own, stages = tile // chunk, shard // chunk, 2 * batches
    je, jo, others = rows_e * q, rows_o * q, max(peers - 1, 1)
    hbm = pl.BlockSpec(memory_space=pltpu.HBM)
    smem = pl.BlockSpec(memory_space=pltpu.SMEM)
    vmem = pl.BlockSpec(memory_space=pltpu.VMEM)
    dma = lambda *shape: pltpu.SemaphoreType.DMA(shape)
    piece = (width, chunk)
    out = jax.ShapeDtypeStruct((1, batches, shard, width), F32)
    scratch = [
        pltpu.VMEM((rows_e, cols_e, tile, twice), BF16),
        pltpu.VMEM((rows_e, cols_e, tile, twice), BF16),
        pltpu.VMEM((rows_o, cols_o, tile, twice), BF16),
        pltpu.VMEM((rows_o, cols_o, tile, twice), BF16),
        pltpu.VMEM((2, batches, shard, width), F32),
        pltpu.VMEM((2, batches, shard, width), F32),
        pltpu.VMEM((stages, je) + piece, BF16),
        pltpu.VMEM((stages, je) + piece, BF16),
        pltpu.VMEM((je,) + piece, BF16),
        pltpu.VMEM((je,) + piece, BF16),
        pltpu.VMEM((je,) + piece, F32),
        pltpu.VMEM((je,) + piece, BF16),
        pltpu.VMEM((batches, je) + piece, BF16),
        pltpu.VMEM((je,) + piece, BF16),
        pltpu.VMEM((2, batches, jo) + piece, BF16),
        pltpu.VMEM((jo,) + piece, F32),
        pltpu.VMEM((others, own) + piece, BF16),
        pltpu.VMEM((stages, others, own) + piece, BF16),
        pltpu.VMEM((own,) + piece, BF16),
        dma(2, rows_e // step_of(rows_e)),
        dma(2, cols_o // step_of(cols_o)),
        dma(2, 2, batches),
        dma(je),
        dma(je),
        dma(stages, je),
        dma(stages, je),
        dma(je),
        dma(batches, je),
        dma(own),
        dma(batches, own),
        dma(others, own),
        dma(stages, others, own),
        dma(others),
        dma(stages, others),
    ]
    return pl.pallas_call(
        sweep_kernel,
        out_shape=[out, out],
        in_specs=[smem] * 2 + [hbm] * 6,
        out_specs=[vmem] * 2,
        scratch_shapes=scratch,
        compiler_params=pltpu.CompilerParams(
            collective_id=0,
            has_side_effects=True,
            vmem_limit_bytes=63 * 1024 * 1024,
        ),
        name="sweep",
    )(
        even_ranks.reshape(-1),
        odd_ranks.reshape(-1),
        even_left,
        even_right,
        odd_left,
        odd_right,
        even_sources,
        odd_sources,
    )


def solution(mesh):
    in_specs = (
        P(None, "layer", "row", "col", None, None),
        P(None, "layer", "row", "col", None, None),
        P(None, "layer", "col", "row", None, None),
        P(None, "layer", "col", "row", None, None),
        P(None, "layer", "row", "col"),
        P(None, "layer", "col", "row"),
        P(None, "layer", None, ("row", "col"), None),
        P(None, "layer", None, ("col", "row"), None),
    )
    out_specs = (P("layer", None, ("row", "col"), None), P("layer", None, ("col", "row"), None))
    return jax.shard_map(
        on_device, mesh=mesh, in_specs=in_specs, out_specs=out_specs, check_vma=False
    )
```

time: 540 us -> 300 us (0.56); the launches traced: 532 us -> 300 us
  Pallas kernels: 503 us -> 292 us
  local copies, waits for them, and re-layouts: 21.7 us -> 7.29 us
  other arithmetic: 6.1 us -> 0 us
    pallas_call x28 -> x1, Pallas kernels: 503 us -> 292 us  [on_device(): pl.pallas_call(sweep_kernel, out_shape=[out, out], in_specs=[smem] * 2 +...]
    unnamed x54 -> x3, local copies, waits for them, and re-layouts: 20.6 us -> 5.29 us
where the time goes in v1:
time: 300 us
  Pallas kernels  292 us (97%)
  local copies, waits for them, and re-layouts  7.29 us (2%)
    pallas_call x1, Pallas kernels, on_device(): pl.pallas_call(sweep_kernel, out_shape=[out, out], in_specs=[smem] * 2 +...  292 us

profile of v1, /device:TPU:7, one launch (start us, length us, event | category | flops | bytes accessed | tf_op | source)
XLA Modules:
  0.0 299.5 jit_solution(16610326704467765202)
XLA Ops:
  0.6 1.3 reshape.11.orank
  2.0 0.8 copy.10
  2.7 0.7 reshape.10.erank
  3.4 291.6 %sweep.1 = (f32[1,2,1024,128]{3,2,1,0:T(8,128)}, f32[1,2,1024,128]{3,2,1,0:T(8,128)}) custom-call(s32[256]{0:T(256)} %reshape.10.erank, s32[256]{0:T(256)} %reshape.11.orank, bf16[2,1,16,8,256,128]{5,4,3,2,1,0:T(8,128)(2,1)} %eleft.1, bf16[2,1,16,8,256,128]{5,4,3,2,1,0:T(8,128)(2,1)} %eright.1, bf16[2,1,8,16,256,128]{5,4,3,2,1,0:T(8,128)(2,1)} %oleft.1, ...), custom_call_target="tpu_custom_call" | custom-call | tf_op jit(solution)/shard_map/sweep/pallas_call | solution.py:520
  295.0 2.3 copy.13
  297.3 2.3 copy.14

commit v2 on v1

v2 whole, which is shorter than its diff:
```python
import functools

import jax
import jax.numpy as jnp
from jax import lax
from jax.experimental import pallas as pl
from jax.experimental.pallas import tpu as pltpu
from jax.sharding import PartitionSpec as P

MESH = pl.DeviceIdType.MESH
F32, BF16 = jnp.float32, jnp.bfloat16


def sizes(right, sources):
    _, _, rows, cols, tile, twice = right.shape
    batches, shard, width = sources.shape[2:]
    return rows, cols, tile, twice, batches, shard, width, min(tile, shard)


def step_of(count):
    return 2 if count % 2 == 0 else 1


def skew_of(count, line):
    return max(1, min(4, (count - 2) // max(line - 1, 1)))


def buffers_of(count, step, line, batches):
    return 1 if skew_of(count, line) * (line - 1) <= count - step else 2, 2 if batches <= 2 else 2 * batches


def sweep_kernel(
    erank, orank, eleft, eright, oleft, oright, esrc, osrc, eout, oout,
    ev, eu, ov, ou, se, so, a_recv, b_recv, a_send, b_send, part, x_local, x_odd, x_hand, x_even,
    stk, acc, rs_send, rs_recv, hand,
    le_sem, lv_sem, lu_sem, src_sem, as_sem, bs_sem, ar_sem, br_sem, us_sem, ur_sem, hs_sem, hr_sem,
    gs_sem, gr_sem, rss_sem, rsr_sem,
):
    rows_e, cols_e, tile, twice, batches, shard, width, chunk = sizes(eright, esrc)
    rows_o, cols_o = oright.shape[2:4]
    half, batch = twice // 2, width // 2
    q = tile // chunk
    own = shard // chunk
    je, jo = rows_e * q, rows_o * q
    pe, po = step_of(rows_e), step_of(cols_o)
    pr = step_of(rows_o)
    segments, peers, line = (lax.axis_size(axis) for axis in ("layer", "row", "col"))
    p, r, i = (lax.axis_index(axis) for axis in ("layer", "row", "col"))
    skew, lag, ends = skew_of(je, line), 2 * po * q, batches * je
    parts, sides = buffers_of(je, pe * q, line, batches)
    first = jnp.where(2 * p <= segments - 1, 0, 1)
    has_e = lambda way: jnp.logical_or(way == 1, p > 0)
    has_o = lambda way: jnp.logical_or(way == 0, p < segments - 1)

    barrier = pltpu.get_barrier_semaphore()
    expect = jnp.int32(peers - 1)
    for k in range(1, peers):
        pl.semaphore_signal(barrier, inc=1, device_id={"row": lax.rem(r + k, peers)}, device_id_type=MESH)
    for axis, at, size in (("col", i, line), ("layer", p, segments)):
        for ok, to in ((at > 0, at - 1), (at < size - 1, at + 1)):

            @pl.when(ok)
            def _(axis=axis, to=to):
                pl.semaphore_signal(barrier, inc=1, device_id={axis: to}, device_id_type=MESH)

            expect = expect + jnp.where(ok, 1, 0)

    def src_copy(parity, way, m):
        ref, buf = ((esrc, se), (osrc, so))[parity]
        return pltpu.make_async_copy(ref.at[way, 0, m], buf.at[way, m], src_sem.at[parity, way, m])

    def load_e(way, t):
        at = pl.ds(t * pe, pe)
        return [
            pltpu.make_async_copy(ref.at[way, 0, at], buf.at[at], le_sem.at[n, t])
            for n, (ref, buf) in enumerate(((eright, ev), (eleft, eu)))
        ]

    def load_v(way, t):
        at = pl.ds(t * po, po)
        return pltpu.make_async_copy(oright.at[way, 0, :, at], ov.at[:, at], lv_sem.at[t])

    def load_u(way, t):
        at = pl.ds(t * pr, pr)
        return pltpu.make_async_copy(oleft.at[way, 0, at], ou.at[at], lu_sem.at[t])

    def load_all(which, way):
        if which == 0:

            @pl.loop(0, rows_e // pe)
            def _(t):
                for copy in load_e(way, t):
                    copy.start()

        else:

            @pl.loop(0, cols_o // po)
            def _(t):
                load_v(way, t).start()

            @pl.loop(0, rows_o // pr)
            def _(t):
                load_u(way, t).start()

    for parity in range(2):
        for way in range(2):
            for m in range(batches):
                src_copy(parity, way, m).start()
    second = 1 - first
    for turn in range(2):
        for which, has in ((0, has_e), (1, has_o)):
            now = (first == which) if turn == 0 else (first != which)

            @pl.when(now & has(first))
            def _(which=which):
                load_all(which, first)

            @pl.when(now & jnp.logical_not(has(first)) & has(second))
            def _(which=which):
                load_all(which, second)

    pl.semaphore_wait(barrier, expect)

    lane = lax.broadcasted_iota(jnp.int32, (1, twice), 1)
    sign = jnp.where(lane < half, 1.0, -1.0).astype(F32)
    within = jnp.where(lane < half, lane, lane - half)

    def stacked_of(coeff, rank):
        mask = (within < rank).astype(F32)
        top = (coeff[:batch] * sign - pltpu.roll(coeff[batch:], half, 1)) * mask
        low = pltpu.roll(top, half, 1) * (-sign)
        return jnp.concatenate([top, low], axis=0).astype(BF16)

    def tile_of(load, t):
        pieces = [load(t * q + n) for n in range(q)]
        return pieces[0] if q == 1 else jnp.concatenate(pieces, axis=1)

    def source_t(buf, way, m, t):
        return buf[way, m, pl.ds(pl.multiple_of(t * chunk, chunk), chunk), :].T

    def keep(out, turn, m, t, value):
        at = pl.ds(pl.multiple_of(t * chunk, chunk), chunk)

        @pl.when(turn == 0)
        def _():
            out[0, m, at, :] = value.T

        @pl.when(turn != 0)
        def _():
            out[0, m, at, :] = out[0, m, at, :] + value.T

    def even_product(way, m, a):
        stacked = [[] for _ in range(pe)]
        for c in range(cols_e):
            right = jnp.concatenate([ev[a + j, c] for j in range(pe)], axis=1)
            x = tile_of(lambda n: x_even[way, m, n], c)
            coeff = jnp.dot(x, right, preferred_element_type=F32)
            for j in range(pe):
                rank = erank[(way * rows_e + a + j) * cols_e + c]
                stacked[j].append(stacked_of(coeff[:, j * twice : (j + 1) * twice], rank))
        for j in range(pe):
            total = lax.dot_general(
                jnp.concatenate(stacked[j], axis=1),
                jnp.concatenate([eu[a + j, c] for c in range(cols_e)], axis=1),
                (((1,), (1,)), ((), ())),
                preferred_element_type=F32,
            )
            for n in range(q):
                part[lax.rem(m, parts), (a + j) * q + n] = total[:, n * chunk : (n + 1) * chunk]

    def odd_columns(way, k, m, t, load):
        @pl.when(m == 0)
        def _():
            load_v(way, t).wait()

        for g in range(po):
            c = t * po + g
            x = tile_of(load, c)
            for a in range(0, rows_o, pr):
                right = jnp.concatenate([ov[a + j, c] for j in range(pr)], axis=1)
                coeff = jnp.dot(x, right, preferred_element_type=F32)
                for j in range(pr):
                    rank = orank[(way * rows_o + a + j) * cols_o + c]
                    stk[way, a + j, c] = stacked_of(coeff[:, j * twice : (j + 1) * twice], rank)

        @pl.when((k == batches - 1) & has_o(second))
        def _():
            load_v(second, t).start()

    def a_copy(k, j):
        return pltpu.make_async_remote_copy(
            src_ref=a_send.at[j], dst_ref=a_recv.at[lax.rem(k, sides), j],
            send_sem=as_sem.at[j], recv_sem=ar_sem.at[lax.rem(k, sides), j],
            device_id={"col": lax.rem(i + 1, line)}, device_id_type=MESH,
        )

    def b_copy(k, j):
        return pltpu.make_async_remote_copy(
            src_ref=b_send.at[j], dst_ref=b_recv.at[lax.rem(k, sides), j],
            send_sem=bs_sem.at[j], recv_sem=br_sem.at[lax.rem(k, sides), j],
            device_id={"col": lax.rem(i + line - 1, line)}, device_id_type=MESH,
        )

    def up_copy(m, j):
        return pltpu.make_async_remote_copy(
            src_ref=x_hand.at[j], dst_ref=x_odd.at[m, j],
            send_sem=us_sem.at[j], recv_sem=ur_sem.at[m, j],
            device_id={"layer": lax.rem(p + segments - 1, segments)}, device_id_type=MESH,
        )

    def down_copy(m, t):
        return pltpu.make_async_remote_copy(
            src_ref=hand.at[t], dst_ref=x_even.at[0, m, r * own + t],
            send_sem=hs_sem.at[t], recv_sem=hr_sem.at[m, t],
            device_id={"layer": lax.rem(p + 1, segments)}, device_id_type=MESH,
        )

    def gather_copy(k, way, m, t, d, source):
        slot = x_even.at[way, m, source * own + t]
        return pltpu.make_async_remote_copy(
            src_ref=slot, dst_ref=slot,
            send_sem=gs_sem.at[d - 1, t], recv_sem=gr_sem.at[k, d - 1, t],
            device_id={"row": lax.rem(r + d, peers)}, device_id_type=MESH,
        )

    def scatter_copy(k, at, d):
        return pltpu.make_async_remote_copy(
            src_ref=rs_send.at[at], dst_ref=rs_recv.at[k, d - 1, lax.rem(at, own)],
            send_sem=rss_sem.at[at], recv_sem=rsr_sem.at[k, d - 1, lax.rem(at, own)],
            device_id={"row": lax.rem(r + d, peers)}, device_id_type=MESH,
        )

    across = (first == 0) & (2 * (p + 1) > segments - 1) & (p < segments - 1)
    behind = jnp.maximum(i, line - 1 - i)

    def sweep_pass(way, turn):
        full = has_e(way)
        final = jnp.logical_and(way == 1, p == 0)
        base = turn * batches

        def sends_a(at, o):
            need = jnp.logical_or(full, at >= o) & (jnp.logical_not(final) | (o > at))
            return need & (at >= 0) & (at < line - 1)

        def sends_b(at, o):
            need = jnp.logical_or(full, at <= o) & (jnp.logical_not(final) | (o < at))
            return need & (at > 0) & (at < line)

        def opening(m):
            k = base + m
            src_copy(0, way, m).wait()
            if way == 1:
                odd_rest(1, k, turn, m)

            @pl.when(full)
            def _():
                for t in range(own):
                    if way == 0:
                        down_copy(m, t).wait_recv()
                        for d in range(1, peers):
                            gather_copy(k, way, m, t, d, r).start()
                if way == 1:
                    keep_odd(turn, m)
                for t in range(own):
                    for d in range(1, peers):
                        gather_copy(k, way, m, t, d, lax.rem(r + peers - d, peers)).wait_recv()
                for t in range(own):
                    for d in range(1, peers):
                        gather_copy(k, way, m, t, d, r).wait_send()

        @pl.loop(0, ends + skew * (line - 1) + lag)
        def _(s):
            @pl.when(s < ends)
            def _():
                m, j = s // je, lax.rem(s, je)
                page = lax.rem(m, parts)

                @pl.when(j == 0)
                def _():
                    opening(m)

                @pl.when(full & (lax.rem(j, pe * q) == 0))
                def _():
                    t = j // (pe * q)

                    @pl.when(m == 0)
                    def _():
                        for copy in load_e(way, t):
                            copy.wait()

                    even_product(way, m, t * pe)

                    @pl.when((turn == 0) & (m == batches - 1) & has_e(second))
                    def _():
                        for copy in load_e(second, t):
                            copy.start()

                    for n in range(pe * q):
                        mine = j + n - i * own

                        @pl.when((mine >= 0) & (mine < own))
                        def _(n=n, mine=mine):
                            part[page, j + n] = part[page, j + n] + source_t(se, way, m, mine)

                @pl.when(jnp.logical_not(full))
                def _():
                    mine = j - i * own
                    part[page, j] = jnp.zeros((width, chunk), F32)

                    @pl.when((mine >= 0) & (mine < own))
                    def _():
                        part[page, j] = source_t(se, way, m, mine)

            ga = s - skew * i

            @pl.when((ga >= 0) & (ga < ends))
            def _():
                m, j = ga // je, lax.rem(ga, je)
                k, page, o = base + m, lax.rem(m, parts), j // own
                got, put = sends_a(i - 1, o), sends_a(i, o)

                @pl.when(got)
                def _():
                    a_copy(k, j).wait_recv()

                @pl.when(put & (m > 0))
                def _():
                    a_copy(k - 1, j).wait_send()

                @pl.when(put & got)
                def _():
                    a_send[j] = (part[page, j] + a_recv[lax.rem(k, sides), j].astype(F32)).astype(BF16)

                @pl.when(put & jnp.logical_not(got))
                def _():
                    a_send[j] = part[page, j].astype(BF16)

                @pl.when(put)
                def _():
                    a_copy(k, j).start()

            gb = s - skew * (line - 1 - i)

            @pl.when((gb >= 0) & (gb < ends))
            def _():
                m, j = gb // je, lax.rem(gb, je)
                k, page, o = base + m, lax.rem(m, parts), j // own
                got, put = sends_b(i + 1, o), sends_b(i, o)

                @pl.when(got)
                def _():
                    b_copy(k, j).wait_recv()

                @pl.when(put & (m > 0))
                def _():
                    b_copy(k - 1, j).wait_send()

                @pl.when(put & got)
                def _():
                    b_send[j] = (part[page, j] + b_recv[lax.rem(k, sides), j].astype(F32)).astype(BF16)

                @pl.when(put & jnp.logical_not(got))
                def _():
                    b_send[j] = part[page, j].astype(BF16)

                @pl.when(put)
                def _():
                    b_copy(k, j).start()

            gt = s - skew * behind

            @pl.when((gt >= 0) & (gt < ends))
            def _():
                m, j = gt // je, lax.rem(gt, je)
                k, page, o = base + m, lax.rem(m, parts), j // own
                mine = o == i

                @pl.when(jnp.logical_not(final) | mine)
                def _():
                    @pl.when(sends_a(i - 1, o))
                    def _():
                        part[page, j] = part[page, j] + a_recv[lax.rem(k, sides), j].astype(F32)

                    @pl.when(sends_b(i + 1, o))
                    def _():
                        part[page, j] = part[page, j] + b_recv[lax.rem(k, sides), j].astype(F32)

                if way == 1:

                    @pl.when(jnp.logical_not(final))
                    def _():
                        @pl.when(m > 0)
                        def _():
                            up_copy(m - 1, j).wait_send()

                        x_hand[j] = part[page, j].astype(BF16)
                        up_copy(m, j).start()

                @pl.when(mine)
                def _():
                    keep(eout, turn, m, j - i * own, part[page, j])

                if way == 0:

                    @pl.when(j == 0)
                    def _():
                        odd_start(0, m)

                    x_local[lax.rem(j, po * q)] = part[page, j].astype(BF16)

                    @pl.when(lax.rem(j, po * q) == po * q - 1)
                    def _():
                        odd_columns(way, k, m, j // (po * q), lambda n: x_local[lax.rem(n, po * q)])

                    @pl.when(j == je - 1)
                    def _():
                        odd_rest(0, k, turn, m)
                        keep_odd(turn, m)

                else:

                    @pl.when((j == 0) & (m < batches - 1))
                    def _():
                        odd_start(1, m + 1)

            if way == 0:
                ju = gt - lag - (batches - 1) * je

                @pl.when((turn == 0) & across & (ju >= 0) & (ju < je) & (lax.rem(ju + je, po * q) == po * q - 1))
                def _():
                    up_columns(base + batches, 0, ju // (po * q))

            else:
                j = lax.rem(s, je)

                @pl.when(has_o(1) & (s < ends - je) & (lax.rem(j, po * q) == po * q - 1))
                def _():
                    up_columns(base + s // je + 1, s // je + 1, j // (po * q))

        last = base + batches - 1

        @pl.loop(0, je)
        def _(j):
            o = j // own

            @pl.when(sends_a(i, o))
            def _():
                a_copy(last, j).wait_send()

            @pl.when(sends_b(i, o))
            def _():
                b_copy(last, j).wait_send()

            if way == 1:

                @pl.when(jnp.logical_not(final))
                def _():
                    up_copy(batches - 1, j).wait_send()

        if way == 0:

            @pl.when(p < segments - 1)
            def _():
                for t in range(own):
                    down_copy(batches - 1, t).wait_send()

    def keep_odd(turn, m):
        for t in range(own):
            keep(oout, turn, m, t, acc[t])

    def up_columns(k, m, t):
        for n in range(po * q):
            up_copy(m, t * po * q + n).wait_recv()
        odd_columns(1, k, m, t, lambda n: x_odd[m, n])

    def odd_start(way, m):
        src_copy(1, way, m).wait()
        for t in range(own):
            acc[t] = source_t(so, way, m, t)

    def odd_rest(way, k, turn, m):
        full = has_o(way)
        begin = (lax.rem(r + 1, peers) * own // (q * pr)) * pr

        @pl.when(full)
        def _():
            @pl.loop(0, rows_o // pr)
            def _(n):
                a = lax.rem(begin + n * pr, rows_o)

                @pl.when(m == 0)
                def _():
                    load_u(way, a // pr).wait()

                totals = [
                    lax.dot_general(
                        jnp.concatenate([stk[way, a + j, c] for c in range(cols_o)], axis=1),
                        jnp.concatenate([ou[a + j, c] for c in range(cols_o)], axis=1),
                        (((1,), (1,)), ((), ())),
                        preferred_element_type=F32,
                    )
                    for j in range(pr)
                ]
                for j in range(pr):
                    for h in range(q):
                        at = (a + j) * q + h
                        owner = at // own
                        value = totals[j][:, h * chunk : (h + 1) * chunk]

                        @pl.when(owner == r)
                        def _(at=at, value=value):
                            mine = at - r * own
                            acc[mine] = acc[mine] + value

                        @pl.when(owner != r)
                        def _(at=at, owner=owner, value=value):
                            rs_send[at] = value.astype(BF16)
                            scatter_copy(k, at, lax.rem(owner + peers - r, peers)).start()

                @pl.when((k == batches - 1) & has_o(second))
                def _():
                    load_u(second, a // pr).start()

            for t in range(own):
                for d in range(1, peers):
                    scatter_copy(k, r * own + t, d).wait_recv()
                    acc[t] = acc[t] + rs_recv[k, d - 1, t].astype(F32)

        for t in range(own):
            if way == 0:

                @pl.when(p < segments - 1)
                def _(t=t):
                    @pl.when(m > 0)
                    def _():
                        down_copy(m - 1, t).wait_send()

                    hand[t] = acc[t].astype(BF16)
                    down_copy(m, t).start()

            else:
                x_even[way, m, r * own + t] = acc[t].astype(BF16)
                for d in range(1, peers):
                    gather_copy(k, way, m, t, d, r).start()

        @pl.when(full)
        def _():
            @pl.loop(0, jo)
            def _(at):
                owner = at // own

                @pl.when(owner != r)
                def _():
                    scatter_copy(k, at, lax.rem(owner + peers - r, peers)).wait_send()

    @pl.loop(0, 2)
    def _(turn):
        way = jnp.where(turn == 0, first, second)

        @pl.when(way == 0)
        def _():
            sweep_pass(0, turn)

        @pl.when(way == 1)
        def _():
            odd_start(1, 0)

            @pl.when(has_o(1) & ((turn == 0) | jnp.logical_not(across)))
            def _():
                @pl.loop(0, cols_o // po)
                def _(t):
                    up_columns(turn * batches, 0, t)

            sweep_pass(1, turn)


def on_device(even_left, even_right, odd_left, odd_right, even_ranks, odd_ranks, even_sources, odd_sources):
    rows_e, cols_e, tile, twice, batches, shard, width, chunk = sizes(even_right, even_sources)
    rows_o, cols_o = odd_right.shape[2:4]
    peers = lax.axis_size("row")
    q, own, stages = tile // chunk, shard // chunk, 2 * batches
    je, jo, others = rows_e * q, rows_o * q, max(peers - 1, 1)
    parts, sides = buffers_of(je, step_of(rows_e) * q, lax.axis_size("col"), batches)
    hbm = pl.BlockSpec(memory_space=pltpu.HBM)
    smem = pl.BlockSpec(memory_space=pltpu.SMEM)
    vmem = pl.BlockSpec(memory_space=pltpu.VMEM)
    dma = lambda *shape: pltpu.SemaphoreType.DMA(shape)
    piece = (width, chunk)
    out = jax.ShapeDtypeStruct((1, batches, shard, width), F32)
    scratch = [
        pltpu.VMEM((rows_e, cols_e, tile, twice), BF16),
        pltpu.VMEM((rows_e, cols_e, tile, twice), BF16),
        pltpu.VMEM((rows_o, cols_o, tile, twice), BF16),
        pltpu.VMEM((rows_o, cols_o, tile, twice), BF16),
        pltpu.VMEM((2, batches, shard, width), F32),
        pltpu.VMEM((2, batches, shard, width), F32),
        pltpu.VMEM((sides, je) + piece, BF16),
        pltpu.VMEM((sides, je) + piece, BF16),
        pltpu.VMEM((je,) + piece, BF16),
        pltpu.VMEM((je,) + piece, BF16),
        pltpu.VMEM((parts, je) + piece, F32),
        pltpu.VMEM((step_of(cols_o) * q,) + piece, BF16),
        pltpu.VMEM((batches, je) + piece, BF16),
        pltpu.VMEM((je,) + piece, BF16),
        pltpu.VMEM((2, batches, jo) + piece, BF16),
        pltpu.VMEM((2, rows_o, cols_o, width, twice), BF16),
        pltpu.VMEM((own,) + piece, F32),
        pltpu.VMEM((jo,) + piece, BF16),
        pltpu.VMEM((stages, others, own) + piece, BF16),
        pltpu.VMEM((own,) + piece, BF16),
        dma(2, rows_e // step_of(rows_e)),
        dma(cols_o // step_of(cols_o)),
        dma(rows_o // step_of(rows_o)),
        dma(2, 2, batches),
        dma(je),
        dma(je),
        dma(sides, je),
        dma(sides, je),
        dma(je),
        dma(batches, je),
        dma(own),
        dma(batches, own),
        dma(others, own),
        dma(stages, others, own),
        dma(jo),
        dma(stages, others, own),
    ]
    return pl.pallas_call(
        sweep_kernel,
        out_shape=[out, out],
        in_specs=[smem] * 2 + [hbm] * 6,
        out_specs=[vmem] * 2,
        scratch_shapes=scratch,
        compiler_params=pltpu.CompilerParams(
            collective_id=0,
            has_side_effects=True,
            vmem_limit_bytes=63 * 1024 * 1024,
        ),
        name="sweep",
    )(
        even_ranks.reshape(-1),
        odd_ranks.reshape(-1),
        even_left,
        even_right,
        odd_left,
        odd_right,
        even_sources,
        odd_sources,
    )


def solution(mesh):
    in_specs = (
        P(None, "layer", "row", "col", None, None),
        P(None, "layer", "row", "col", None, None),
        P(None, "layer", "col", "row", None, None),
        P(None, "layer", "col", "row", None, None),
        P(None, "layer", "row", "col"),
        P(None, "layer", "col", "row"),
        P(None, "layer", None, ("row", "col"), None),
        P(None, "layer", None, ("col", "row"), None),
    )
    out_specs = (P("layer", None, ("row", "col"), None), P("layer", None, ("col", "row"), None))
    return jax.shard_map(
        on_device, mesh=mesh, in_specs=in_specs, out_specs=out_specs, check_vma=False
    )
```

time: 300 us -> 249 us (0.83)
  Pallas kernels: 292 us -> 241 us
    pallas_call x1, Pallas kernels: 292 us -> 241 us  [on_device(): pl.pallas_call(sweep_kernel, out_shape=[out, out], in_specs=[smem] * 2 +...]
where the time goes in v2:
time: 249 us
  Pallas kernels  241 us (97%)
  local copies, waits for them, and re-layouts  7.29 us (3%)
    pallas_call x1, Pallas kernels, on_device(): pl.pallas_call(sweep_kernel, out_shape=[out, out], in_specs=[smem] * 2 +...  241 us
    unnamed x3, local copies, waits for them, and re-layouts  5.29 us

profile of v2, /device:TPU:7, one launch (start us, length us, event | category | flops | bytes accessed | tf_op | source)
XLA Modules:
  0.0 248.6 jit_solution(12512346268585241567)
XLA Ops:
  0.6 1.3 reshape.11.orank
  2.0 0.8 copy.10
  2.7 0.7 reshape.10.erank
  3.4 240.7 %sweep.1 = (f32[1,2,1024,128]{3,2,1,0:T(8,128)}, f32[1,2,1024,128]{3,2,1,0:T(8,128)}) custom-call(s32[256]{0:T(256)} %reshape.10.erank, s32[256]{0:T(256)} %reshape.11.orank, bf16[2,1,16,8,256,128]{5,4,3,2,1,0:T(8,128)(2,1)} %eleft.1, bf16[2,1,16,8,256,128]{5,4,3,2,1,0:T(8,128)(2,1)} %eright.1, bf16[2,1,8,16,256,128]{5,4,3,2,1,0:T(8,128)(2,1)} %oleft.1, ...), custom_call_target="tpu_custom_call" | custom-call | tf_op jit(solution)/shard_map/sweep/pallas_call | solution.py:628
  244.1 2.3 copy.13
  246.3 2.3 copy.14

commit v3 on v2

--- a/solution.py
+++ b/solution.py
@@ -32,7 +32,7 @@
 def sweep_kernel(
     erank, orank, eleft, eright, oleft, oright, esrc, osrc, eout, oout,
     ev, eu, ov, ou, se, so, a_recv, b_recv, a_send, b_send, part, x_local, x_odd, x_hand, x_even,
-    stk, acc, rs_send, rs_recv, hand,
+    stk, sums, acc, rs_send, rs_recv,
     le_sem, lv_sem, lu_sem, src_sem, as_sem, bs_sem, ar_sem, br_sem, us_sem, ur_sem, hs_sem, hr_sem,
     gs_sem, gr_sem, rss_sem, rsr_sem,
 ):
@@ -48,6 +48,7 @@
     p, r, i = (lax.axis_index(axis) for axis in ("layer", "row", "col"))
     skew, lag, ends = skew_of(je, line), 2 * po * q, batches * je
     parts, sides = buffers_of(je, pe * q, line, batches)
+    early = max(cols_o // po * 3 // 4, 1)
     first = jnp.where(2 * p <= segments - 1, 0, 1)
     has_e = lambda way: jnp.logical_or(way == 1, p > 0)
     has_o = lambda way: jnp.logical_or(way == 0, p < segments - 1)
@@ -168,6 +169,17 @@
             for n in range(q):
                 part[lax.rem(m, parts), (a + j) * q + n] = total[:, n * chunk : (n + 1) * chunk]
 
+    def contract(way, a, columns):
+        return [
+            lax.dot_general(
+                jnp.concatenate([stk[way, a + j, c] for c in columns], axis=1),
+                jnp.concatenate([ou[a + j, c] for c in columns], axis=1),
+                (((1,), (1,)), ((), ())),
+                preferred_element_type=F32,
+            )
+            for j in range(pr)
+        ]
+
     def odd_columns(way, k, m, t, load):
         @pl.when(m == 0)
         def _():
@@ -187,6 +199,18 @@
         def _():
             load_v(second, t).start()
 
+        @pl.when(t == early - 1)
+        def _():
+            @pl.loop(0, rows_o // pr)
+            def _(n):
+                @pl.when(m == 0)
+                def _():
+                    load_u(way, n).wait()
+
+                for j, total in enumerate(contract(way, n * pr, range(early * po))):
+                    for h in range(q):
+                        sums[(n * pr + j) * q + h] = total[:, h * chunk : (h + 1) * chunk]
+
     def a_copy(k, j):
         return pltpu.make_async_remote_copy(
             src_ref=a_send.at[j], dst_ref=a_recv.at[lax.rem(k, sides), j],
@@ -210,7 +234,7 @@
 
     def down_copy(m, t):
         return pltpu.make_async_remote_copy(
-            src_ref=hand.at[t], dst_ref=x_even.at[0, m, r * own + t],
+            src_ref=rs_send.at[r * own + t], dst_ref=x_even.at[0, m, r * own + t],
             send_sem=hs_sem.at[t], recv_sem=hr_sem.at[m, t],
             device_id={"layer": lax.rem(p + 1, segments)}, device_id_type=MESH,
         )
@@ -225,7 +249,7 @@
 
     def scatter_copy(k, at, d):
         return pltpu.make_async_remote_copy(
-            src_ref=rs_send.at[at], dst_ref=rs_recv.at[k, d - 1, lax.rem(at, own)],
+            src_ref=rs_send.at[at], dst_ref=rs_recv.at[lax.rem(k, sides), d - 1, lax.rem(at, own)],
             send_sem=rss_sem.at[at], recv_sem=rsr_sem.at[k, d - 1, lax.rem(at, own)],
             device_id={"row": lax.rem(r + d, peers)}, device_id_type=MESH,
         )
@@ -488,24 +512,13 @@
             def _(n):
                 a = lax.rem(begin + n * pr, rows_o)
 
-                @pl.when(m == 0)
-                def _():
-                    load_u(way, a // pr).wait()
-
-                totals = [
-                    lax.dot_general(
-                        jnp.concatenate([stk[way, a + j, c] for c in range(cols_o)], axis=1),
-                        jnp.concatenate([ou[a + j, c] for c in range(cols_o)], axis=1),
-                        (((1,), (1,)), ((), ())),
-                        preferred_element_type=F32,
-                    )
-                    for j in range(pr)
-                ]
+                rest = range(early * po, cols_o)
+                totals = contract(way, a, rest) if len(rest) else [jnp.zeros((width, tile), F32)] * pr
                 for j in range(pr):
                     for h in range(q):
                         at = (a + j) * q + h
                         owner = at // own
-                        value = totals[j][:, h * chunk : (h + 1) * chunk]
+                        value = totals[j][:, h * chunk : (h + 1) * chunk] + sums[at]
 
                         @pl.when(owner == r)
                         def _(at=at, value=value):
@@ -524,7 +537,7 @@
             for t in range(own):
                 for d in range(1, peers):
                     scatter_copy(k, r * own + t, d).wait_recv()
-                    acc[t] = acc[t] + rs_recv[k, d - 1, t].astype(F32)
+                    acc[t] = acc[t] + rs_recv[lax.rem(k, sides), d - 1, t].astype(F32)
 
         for t in range(own):
             if way == 0:
@@ -535,7 +548,7 @@
                     def _():
                         down_copy(m - 1, t).wait_send()
 
-                    hand[t] = acc[t].astype(BF16)
+                    rs_send[r * own + t] = acc[t].astype(BF16)
                     down_copy(m, t).start()
 
             else:
@@ -604,10 +617,10 @@
         pltpu.VMEM((je,) + piece, BF16),
         pltpu.VMEM((2, batches, jo) + piece, BF16),
         pltpu.VMEM((2, rows_o, cols_o, width, twice), BF16),
+        pltpu.VMEM((jo,) + piece, F32),
         pltpu.VMEM((own,) + piece, F32),
         pltpu.VMEM((jo,) + piece, BF16),
-        pltpu.VMEM((stages, others, own) + piece, BF16),
-        pltpu.VMEM((own,) + piece, BF16),
+        pltpu.VMEM((sides, others, own) + piece, BF16),
         dma(2, rows_e // step_of(rows_e)),
         dma(cols_o // step_of(cols_o)),
         dma(rows_o // step_of(rows_o)),
@@ -634,7 +647,7 @@
         compiler_params=pltpu.CompilerParams(
             collective_id=0,
             has_side_effects=True,
-            vmem_limit_bytes=63 * 1024 * 1024,
+            vmem_limit_bytes=67_000_320,
         ),
         name="sweep",
     )(

time: 249 us -> 246 us (0.988)
  Pallas kernels: 241 us -> 238 us
    pallas_call x1, Pallas kernels: 241 us -> 238 us  [on_device(): pl.pallas_call(sweep_kernel, out_shape=[out, out], in_specs=[smem] * 2 +...]
where the time goes in v3:
time: 246 us
  Pallas kernels  238 us (97%)
  local copies, waits for them, and re-layouts  7.29 us (3%)
    pallas_call x1, Pallas kernels, on_device(): pl.pallas_call(sweep_kernel, out_shape=[out, out], in_specs=[smem] * 2 +...  238 us
    unnamed x3, local copies, waits for them, and re-layouts  5.29 us

profile of v3, /device:TPU:7, one launch (start us, length us, event | category | flops | bytes accessed | tf_op | source)
XLA Modules:
  0.0 245.6 jit_solution(4579273437603627437)
XLA Ops:
  0.6 1.3 reshape.11.orank
  2.0 0.8 copy.10
  2.7 0.7 reshape.10.erank
  3.4 237.7 %sweep.1 = (f32[1,2,1024,128]{3,2,1,0:T(8,128)}, f32[1,2,1024,128]{3,2,1,0:T(8,128)}) custom-call(s32[256]{0:T(256)} %reshape.10.erank, s32[256]{0:T(256)} %reshape.11.orank, bf16[2,1,16,8,256,128]{5,4,3,2,1,0:T(8,128)(2,1)} %eleft.1, bf16[2,1,16,8,256,128]{5,4,3,2,1,0:T(8,128)(2,1)} %eright.1, bf16[2,1,8,16,256,128]{5,4,3,2,1,0:T(8,128)(2,1)} %oleft.1, ...), custom_call_target="tpu_custom_call" | custom-call | tf_op jit(solution)/shard_map/sweep/pallas_call | solution.py:641
  241.1 2.3 copy.13
  243.4 2.3 copy.14
